TPU v7x, 32 devices: a whole 2x2x4 slice. The times are simulated.
32 devices in a mesh: ctx: 8 (over z, y), tp: 4 (over x, core).
Axes of the slice: x: 2, y: 2, z: 4, core: 2. Of those that a mesh axis runs over, the one named last changes fastest.
Arguments:
- qkv: bfloat16 [1024, 3, 8192], P(('ctx', 'tp')), may hold values from -6 to 6
- filters: float32 [3, 7, 8192], P(None, None, 'tp'), may hold values from -1.5 to 1.5
- doc_ids: int32 [8], replicated, may hold values from 0 to 1, never falling along the last dimension, each value on 1 to 5 neighbouring positions
- upstream: bfloat16 [1024, 8192], P('ctx', 'tp'), may hold values from -6 to 6
Outputs:
- attended: bfloat16 [1024, 8192], P('ctx', 'tp')
- qkv_grad: bfloat16 [1024, 3, 8192], P(('ctx', 'tp'))
- filter_grad: float32 [3, 7, 8192], P(None, None, 'tp')
Inputs may be any that keep to these rules, and one draw needn't show every extreme that they name: doc_ids never falls along the sequence; every document covers 1 to 5 whole blocks of 128 tokens.
All inputs are finite; a program needn't handle non-finite values.
Results may differ from a plain program's by a relative error of at most 0.014.
The roundings to bfloat16 on the way count: a program that leaves them out, or rounds other values in their place, can miss the bound.
Values may be sent and summed in bfloat16 or wider, within the bound.
No kernel may reach another device: no remote copies, remote signals or barrier semaphores. Data moves between devices by JAX's collectives and lax.ppermute only.
A program may use at most 128 MiB of HBM per device.

v0:
```python
import jax
import jax.numpy as jnp
from jax import lax
from jax.sharding import PartitionSpec as P

HEAD_DIM = 128
KW = 7
BLOCK = 128
STEPS = 4


def from_behind(value, axis, steps):
    count = lax.axis_size(axis)
    first, last = (max(0, -steps), min(count, count - steps))
    return lax.ppermute(value, axis, [(source, source + steps) for source in range(first, last)])


def block_docs(doc_ids, first_block, count):
    start = jnp.maximum(first_block, 0)
    picked = lax.dynamic_slice_in_dim(doc_ids, start, count)
    return jnp.repeat(picked, BLOCK)


def shards(qkv, filters, doc_ids, upstream):
    local = lax.all_to_all(qkv, "tp", split_axis=2, concat_axis=0, tiled=True)
    tokens = local.shape[0]
    width = local.shape[2]
    heads = width // HEAD_DIM
    blocks_here = tokens // BLOCK
    logit_scale = HEAD_DIM ** (-0.5)
    position = lax.axis_index("ctx")
    reach = STEPS + 1
    rim = from_behind(local[tokens - (KW - 1) :], "ctx", 1)
    inputs = jnp.concatenate([rim, local], axis=0).astype(jnp.float32)
    mixed = sum(
        (filters[:, lag, :] * inputs[KW - 1 - lag : KW - 1 - lag + tokens] for lag in range(KW))
    )
    mixed = mixed.astype(jnp.bfloat16)
    queries = mixed[:, 0].reshape(tokens, heads, HEAD_DIM)
    key_value = mixed[:, 1:3]
    tiles = [key_value]
    current = key_value
    for distance in range(1, STEPS + 1):
        current = from_behind(current, "ctx", 1)
        tiles.append(current)
    joined = jnp.concatenate(tiles, axis=0)
    keys = joined[:, 0].reshape(reach * tokens, heads, HEAD_DIM)
    values = joined[:, 1].reshape(reach * tokens, heads, HEAD_DIM)
    rows = jnp.arange(tokens)
    query_token = position * tokens + rows
    query_doc = block_docs(doc_ids, position * blocks_here, blocks_here)
    key_tokens = jnp.concatenate(
        [(position - distance) * tokens + rows for distance in range(reach)]
    )
    key_docs = jnp.concatenate(
        [
            block_docs(doc_ids, (position - distance) * blocks_here, blocks_here)
            for distance in range(reach)
        ]
    )
    allowed = (
        (key_tokens[None, :] >= 0)
        & (key_tokens[None, :] <= query_token[:, None])
        & (key_docs[None, :] == query_doc[:, None])
    )
    raw = (
        jnp.einsum("qhd,khd->hqk", queries, keys, preferred_element_type=jnp.float32) * logit_scale
    )
    masked = jnp.where(allowed[None], raw, -1e30)
    row_max = masked.max(axis=2)
    expo = jnp.where(allowed[None], jnp.exp(masked - row_max[:, :, None]), 0.0)
    row_sum = expo.sum(axis=2)
    weighted_values = jnp.einsum(
        "hqk,khd->qhd", expo.astype(jnp.bfloat16), values, preferred_element_type=jnp.float32
    )
    attended = (weighted_values / row_sum.T[:, :, None]).astype(jnp.bfloat16)
    grad_out = upstream.reshape(tokens, heads, HEAD_DIM)
    delta = jnp.sum(grad_out.astype(jnp.float32) * attended.astype(jnp.float32), axis=-1).T
    prob = expo / row_sum[:, :, None]
    value_part = jnp.einsum(
        "hqk,qhd->khd", prob.astype(jnp.bfloat16), grad_out, preferred_element_type=jnp.float32
    )
    probability_gradient = jnp.einsum(
        "qhd,khd->hqk", grad_out, values, preferred_element_type=jnp.float32
    )
    score_gradient = (prob * (probability_gradient - delta[:, :, None]) * logit_scale).astype(
        jnp.bfloat16
    )
    query_gradient_rows = jnp.einsum(
        "hqk,khd->qhd", score_gradient, keys, preferred_element_type=jnp.float32
    )
    key_part = jnp.einsum(
        "hqk,qhd->khd", score_gradient, queries, preferred_element_type=jnp.float32
    )
    stacked = jnp.stack(
        [key_part.reshape(reach, tokens, width), value_part.reshape(reach, tokens, width)], axis=2
    )
    partials = [stacked[distance] for distance in range(reach)]
    carried = partials[STEPS]
    for distance in range(STEPS - 1, -1, -1):
        carried = from_behind(carried, "ctx", -1)
        carried = carried + partials[distance]
    conv_grad = jnp.concatenate([query_gradient_rows.reshape(tokens, 1, width), carried], axis=1)
    grad_edge = from_behind(conv_grad[: KW - 1], "ctx", -1)
    extended = jnp.concatenate([conv_grad, grad_edge], axis=0)
    input_grad = sum((filters[:, lag, :] * extended[lag : lag + tokens] for lag in range(KW)))
    tap_terms = jnp.stack(
        [
            jnp.sum(inputs[KW - 1 - lag : KW - 1 - lag + tokens] * conv_grad, axis=0)
            for lag in range(KW)
        ],
        axis=1,
    )
    filter_grad = lax.psum(tap_terms, "ctx")
    qkv_grad = lax.all_to_all(
        input_grad.astype(jnp.bfloat16), "tp", split_axis=0, concat_axis=2, tiled=True
    )
    return (attended.reshape(tokens, width), qkv_grad, filter_grad)


def solution(mesh):
    return jax.shard_map(
        shards,
        mesh=mesh,
        in_specs=(P(("ctx", "tp"), None, None), P(None, None, "tp"), P(), P("ctx", "tp")),
        out_specs=(P("ctx", "tp"), P(("ctx", "tp"), None, None), P(None, None, "tp")),
        check_vma=False,
    )
```

profile of v0, /device:TPU:0, one launch (start us, length us, event | category | flops | bytes accessed | tf_op | source)
XLA Modules:
  0.0 541.6 jit_solution(776772498163065581)
XLA Ops:
  7.2 10.7 %copy.57 = bf16[32,3,8192]{0,1,2:T(4,128)(2,1)} copy(bf16[32,3,8192]{2,0,1:T(8,128)(2,1)} %param.4) | data formatting | bytes 3145728 | tf_op args[0]
  17.8 8.4 %reshape.158 = bf16[4,2,98304]{2,1,0:T(2,128)(2,1)} reshape(bf16[8192,3,32]{2,1,0:T(4,128)(2,1)} %bitcast.114) | data formatting | bytes 3145728
  26.2 4.3 all-to-all-start
  30.7 19.9 %all-to-all-done = bf16[4,2,98304]{2,1,0:T(2,128)(2,1)S(1)} async-done(((bf16[4,2,98304]{2,1,0:T(2,128)(2,1)}), bf16[4,2,98304]{2,1,0:T(2,128)(2,1)S(1)}, u32[]{:S(2)}, u32[]{:S(2)}) %all-to-all-start) | async-done | bytes 1572896 | tf_op jit(solution)/shard_map/all_to_all | solution.py:25
  50.6 7.1 %reshape.159 = bf16[8192,3,32]{2,1,0:T(4,128)(2,1)} reshape(bf16[4,2,98304]{2,1,0:T(2,128)(2,1)S(1)} %all-to-all-done) | data formatting | bytes 3145728
  57.7 10.5 %copy.59 = bf16[4,32,3,2048]{3,1,0,2:T(8,128)(2,1)S(1)} copy(bf16[4,32,3,2048]{1,2,3,0:T(4,128)(2,1)} %bitcast.113) | data formatting | bytes 3145728 | tf_op jit(solution)/shard_map/all_to_all | solution.py:25
  68.2 4.2 collective-permute-start
  72.5 2.1 collective-permute-done
  74.7 1.9 maximum_convert_fusion
  76.6 2.6 add_convert_fusion
  81.5 5.3 collective-permute-start.1
  86.8 20.0 %collective-permute-done.1 = bf16[128,2,2048]{2,0,1:T(8,128)(2,1)} collective-permute-done((bf16[128,2,2048]{2,0,1:T(8,128)(2,1)S(1)}, bf16[128,2,2048]{2,0,1:T(8,128)(2,1)}, u32[]{:S(2)}, u32[]{:S(2)}) %collective-permute-start.1) | collective-permute-done | bytes 1048608 | tf_op jit(solution)/shard_map/ppermute | solution.py:15
  106.8 5.5 %collective-permute-start.2 = (bf16[128,2,2048]{2,0,1:T(8,128)(2,1)}, bf16[128,2,2048]{2,0,1:T(8,128)(2,1)}, u32[]{:S(2)}, u32[]{:S(2)}) collective-permute-start(bf16[128,2,2048]{2,0,1:T(8,128)(2,1)} %collective-permute-done.1), channel_id=1, source_target_pairs={{0,4},{4,8},{8,12},{12,16},{16,20},{20,24},{24,28},{1,5},{5,9},{9,... | collective-permute-start | bytes 3145736 | tf_op jit(solution)/shard_map/ppermute | solution.py:15
  112.8 19.0 %collective-permute-done.2 = bf16[128,2,2048]{2,0,1:T(8,128)(2,1)} collective-permute-done((bf16[128,2,2048]{2,0,1:T(8,128)(2,1)}, bf16[128,2,2048]{2,0,1:T(8,128)(2,1)}, u32[]{:S(2)}, u32[]{:S(2)}) %collective-permute-start.2) | collective-permute-done | bytes 1048608 | tf_op jit(solution)/shard_map/ppermute | solution.py:15
  131.8 6.2 %collective-permute-start.3 = (bf16[128,2,2048]{2,0,1:T(8,128)(2,1)}, bf16[128,2,2048]{2,0,1:T(8,128)(2,1)}, u32[]{:S(2)}, u32[]{:S(2)}) collective-permute-start(bf16[128,2,2048]{2,0,1:T(8,128)(2,1)} %collective-permute-done.2), channel_id=1, source_target_pairs={{0,4},{4,8},{8,12},{12,16},{16,20},{20,24},{24,28},{1,5},{5,9},{9,... | collective-permute-start | bytes 3145736 | tf_op jit(solution)/shard_map/ppermute | solution.py:15
  141.8 14.7 %collective-permute-done.3 = bf16[128,2,2048]{2,0,1:T(8,128)(2,1)} collective-permute-done((bf16[128,2,2048]{2,0,1:T(8,128)(2,1)}, bf16[128,2,2048]{2,0,1:T(8,128)(2,1)}, u32[]{:S(2)}, u32[]{:S(2)}) %collective-permute-start.3) | collective-permute-done | bytes 1048608 | tf_op jit(solution)/shard_map/ppermute | solution.py:15
  156.5 6.3 %collective-permute-start.4 = (bf16[128,2,2048]{2,0,1:T(8,128)(2,1)}, bf16[128,2,2048]{2,0,1:T(8,128)(2,1)}, u32[]{:S(2)}, u32[]{:S(2)}) collective-permute-start(bf16[128,2,2048]{2,0,1:T(8,128)(2,1)} %collective-permute-done.3), channel_id=1, source_target_pairs={{0,4},{4,8},{8,12},{12,16},{16,20},{20,24},{24,28},{1,5},{5,9},{9,... | collective-permute-start | bytes 3145736 | tf_op jit(solution)/shard_map/ppermute | solution.py:15
  163.5 2.0 copy.65
  168.8 2.0 copy.61
  170.8 2.3 constant_dynamic-update-slice_fusion.3
  173.1 2.3 constant_dynamic-update-slice_fusion.2
  175.4 2.3 constant_dynamic-update-slice_fusion.1
  177.8 2.6 collective-permute-done.4
  180.4 2.3 constant_dynamic-update-slice_fusion
  182.7 5.7 %fusion.48 = (bf16[640,1,2048]{2,0,1:T(8,128)(2,1)}, bf16[640,1,2048]{2,0,1:T(8,128)(2,1)}) fusion(bf16[640,2,2048]{2,0,1:T(8,128)(2,1)} %constant_dynamic-update-slice_fusion), kind=kLoop, calls=%fused_computation.106 | loop fusion | bytes 10485760 | tf_op jit(solution)/shard_map/slice | solution.py:47
  188.4 4.4 copy.62
  192.8 4.5 copy.60
  197.2 6.6 %fusion.52 = (f32[16,128]{1,0:T(8,128)S(1)}, f32[16,128,640]{2,1,0:T(8,128)}) fusion(pred[128,640]{1,0:T(8,128)(4,1)} %and_and_fusion, bf16[128,16,128]{0,2,1:T(8,128)(2,1)} %bitcast.124, bf16[640,16,128]{0,2,1:T(8,128)(2,1)} %bitcast.115), kind=kOutput, calls=%fused_computation.110 | convolution fusion | flops 342098560 | bytes 8478720 | tf_op jit(solution)/shard_map/sub | solution.py:71
  203.8 4.1 fusion.18
  210.7 2.6 fusion.2
  213.3 5.3 copy.72
  218.6 6.8 %stack_reshape.7 = f32[5,128,1,2048]{3,1,0,2:T(8,128)} reshape(f32[640,16,128]{2,1,0:T(8,128)} %copy.72) | data formatting | bytes 10485760 | tf_op jit(solution)/shard_map/stack;reshape | solution.py:95
  225.4 5.0 convolution_bitcast_fusion
  230.5 7.4 %reshape.152 = f32[5,128,1,2048]{1,0,3,2:T(8,128)} reshape(f32[640,16,128]{0,2,1:T(8,128)} %convolution_bitcast_fusion) | data formatting | bytes 10485760 | tf_op jit(solution)/shard_map/stack;reshape | solution.py:95
  237.8 7.9 %copy.73 = f32[5,128,1,2048]{3,1,2,0:T(8,128)} copy(f32[5,128,1,2048]{1,0,3,2:T(8,128)} %reshape.152) | data formatting | bytes 10485760 | tf_op jit(solution)/shard_map/stack;reshape | solution.py:95
  249.1 44.7 %collective-permute-done.5 = f32[128,2,2048]{2,0,1:T(8,128)S(1)} collective-permute-done((f32[128,2,2048]{2,0,1:T(8,128)S(1)}, f32[128,2,2048]{2,0,1:T(8,128)S(1)}, u32[]{:S(2)}, u32[]{:S(2)}) %collective-permute-start.5) | collective-permute-done | bytes 2097184 | tf_op jit(solution)/shard_map/ppermute | solution.py:15
  295.7 44.1 %collective-permute-done.6 = f32[128,2,2048]{2,0,1:T(8,128)S(1)} collective-permute-done((f32[128,2,2048]{2,0,1:T(8,128)S(1)}, f32[128,2,2048]{2,0,1:T(8,128)S(1)}, u32[]{:S(2)}, u32[]{:S(2)}) %collective-permute-start.6) | collective-permute-done | bytes 2097184 | tf_op jit(solution)/shard_map/ppermute | solution.py:15
  341.7 42.9 %collective-permute-done.7 = f32[128,2,2048]{2,0,1:T(8,128)S(1)} collective-permute-done((f32[128,2,2048]{2,0,1:T(8,128)S(1)}, f32[128,2,2048]{2,0,1:T(8,128)S(1)}, u32[]{:S(2)}, u32[]{:S(2)}) %collective-permute-start.7) | collective-permute-done | bytes 2097184 | tf_op jit(solution)/shard_map/ppermute | solution.py:15
  387.4 2.1 fusion.53
  389.5 2.5 copy.75
  392.0 37.3 %collective-permute-done.8 = f32[128,2,2048]{2,0,1:T(8,128)} collective-permute-done((f32[128,2,2048]{2,0,1:T(8,128)}, f32[128,2,2048]{2,0,1:T(8,128)}, u32[]{:S(2)}, u32[]{:S(2)}) %collective-permute-start.8) | collective-permute-done | bytes 2097184 | tf_op jit(solution)/shard_map/ppermute | solution.py:15
  429.4 2.5 fusion.33
  431.9 3.6 multiply_reduce_fusion
  437.5 6.2 %collective-permute-done.9 = f32[6,3,2048]{2,0,1:T(8,128)S(1)} collective-permute-done((f32[6,3,2048]{2,0,1:T(8,128)S(1)}, f32[6,3,2048]{2,0,1:T(8,128)S(1)}, u32[]{:S(2)}, u32[]{:S(2)}) %collective-permute-start.9) | collective-permute-done | bytes 147488 | tf_op jit(solution)/shard_map/ppermute | solution.py:15
  444.2 2.6 fusion.5
  446.9 2.7 copy.76
  449.5 3.7 all-to-all-start.1
  456.3 74.4 %all-reduce.2.cloned.1.call-done = f32[3,7,2048]{2,0,1:T(4,128)} async-done(((f32[3,7,2048]{2,0,1:T(4,128)}), f32[3,7,2048]{2,0,1:T(4,128)}) %all-reduce.2.cloned.1.call-update) | async-done | bytes 172048 | tf_op jit(solution)/shard_map/psum | solution.py:114
  (91 shorter events, 32.8 us)
Async XLA Ops:
  26.2 4.3 copy-start.13
  26.2 24.4 %all-to-all-start = ((bf16[4,2,98304]{2,1,0:T(2,128)(2,1)}), bf16[4,2,98304]{2,1,0:T(2,128)(2,1)S(1)}, u32[]{:S(2)}, u32[]{:S(2)}) async-start(bf16[4,2,98304]{2,1,0:T(2,128)(2,1)} %reshape.158), calls=%async_computation | async-start | bytes 3145728 | tf_op jit(solution)/shard_map/all_to_all | solution.py:25
  68.2 4.3 copy-start.5
  68.2 6.4 %collective-permute-start = (bf16[6,3,2048]{2,0,1:T(8,128)(2,1)S(1)}, bf16[6,3,2048]{2,0,1:T(8,128)(2,1)S(1)}, u32[]{:S(2)}, u32[]{:S(2)}) collective-permute-start(bf16[6,3,2048]{2,0,1:T(8,128)(2,1)S(1)} %slice.138), channel_id=1, source_target_pairs={{0,4},{4,8},{8,12},{12,16},{16,20},{20,24},{24,28},{1,5},{5,9},{9,... | collective-permute-start | bytes 221192 | tf_op jit(solution)/shard_map/ppermute | solution.py:15
  72.5 6.7 %copy-start.11 = (f32[3,1,2048]{2,0,1:T(4,128)}, f32[3,1,2048]{2,0,1:T(4,128)S(1)}, u32[]{:S(2)}) copy-start(f32[3,1,2048]{2,0,1:T(4,128)S(1)} %copy.107) | copy-start | bytes 73732
  79.2 1.1 copy-start.6
  80.4 57.7 %copy-start.17 = (s32[8]{0:T(128)S(1)}, s32[8]{0:T(128)}, u32[]{:S(2)}) copy-start(s32[8]{0:T(128)} %param.6) | copy-start | bytes 100
  81.5 25.4 %collective-permute-start.1 = (bf16[128,2,2048]{2,0,1:T(8,128)(2,1)S(1)}, bf16[128,2,2048]{2,0,1:T(8,128)(2,1)}, u32[]{:S(2)}, u32[]{:S(2)}) collective-permute-start(bf16[128,2,2048]{2,0,1:T(8,128)(2,1)S(1)} %get-tuple-element.24), channel_id=1, source_target_pairs={{0,4},{4,8},{8,12},{12,16},{16,20},{20,24},{24,28},{1,5},{5,9},{9,... | collective-permute-start | bytes 3145736 | tf_op jit(solution)/shard_map/ppermute | solution.py:15
  106.8 24.9 %collective-permute-start.2 = (bf16[128,2,2048]{2,0,1:T(8,128)(2,1)}, bf16[128,2,2048]{2,0,1:T(8,128)(2,1)}, u32[]{:S(2)}, u32[]{:S(2)}) collective-permute-start(bf16[128,2,2048]{2,0,1:T(8,128)(2,1)} %collective-permute-done.1), channel_id=1, source_target_pairs={{0,4},{4,8},{8,12},{12,16},{16,20},{20,24},{24,28},{1,5},{5,9},{9,... | collective-permute-start | bytes 3145736 | tf_op jit(solution)/shard_map/ppermute | solution.py:15
  131.8 24.7 %collective-permute-start.3 = (bf16[128,2,2048]{2,0,1:T(8,128)(2,1)}, bf16[128,2,2048]{2,0,1:T(8,128)(2,1)}, u32[]{:S(2)}, u32[]{:S(2)}) collective-permute-start(bf16[128,2,2048]{2,0,1:T(8,128)(2,1)} %collective-permute-done.2), channel_id=1, source_target_pairs={{0,4},{4,8},{8,12},{12,16},{16,20},{20,24},{24,28},{1,5},{5,9},{9,... | collective-permute-start | bytes 3145736 | tf_op jit(solution)/shard_map/ppermute | solution.py:15
  156.5 23.9 %collective-permute-start.4 = (bf16[128,2,2048]{2,0,1:T(8,128)(2,1)}, bf16[128,2,2048]{2,0,1:T(8,128)(2,1)}, u32[]{:S(2)}, u32[]{:S(2)}) collective-permute-start(bf16[128,2,2048]{2,0,1:T(8,128)(2,1)} %collective-permute-done.3), channel_id=1, source_target_pairs={{0,4},{4,8},{8,12},{12,16},{16,20},{20,24},{24,28},{1,5},{5,9},{9,... | collective-permute-start | bytes 3145736 | tf_op jit(solution)/shard_map/ppermute | solution.py:15
  203.8 4.1 copy-start.4
  203.8 5.0 copy-start.7
  203.8 5.0 copy-start.9
  245.7 48.1 %slice-start = ((s8[5242880]{0:T(1024)(128)(4,1)}), s8[4194304]{0:T(1024)(128)(4,1)S(1)}, s32[]{:S(2)}) async-start(s8[5242880]{0:T(1024)(128)(4,1)} %bitcast.108), calls=%async_computation.3 | async-start | bytes 8388608
  245.7 48.1 %slice-start.1 = ((s8[5242880]{0:T(1024)(128)(4,1)}), s8[1048576]{0:T(1024)(128)(4,1)S(1)}, s32[]{:S(2)}) async-start(s8[5242880]{0:T(1024)(128)(4,1)} %bitcast.108), calls=%async_computation.4 | async-start | bytes 2097152
  245.7 48.1 %copy-start = (f32[5,128,1,2048]{3,1,2,0:T(8,128)S(1)}, f32[5,128,1,2048]{3,1,2,0:T(8,128)}, u32[]{:S(2)}) copy-start(f32[5,128,1,2048]{3,1,2,0:T(8,128)} %copy.73) | copy-start | bytes 15728644
  247.5 46.3 %collective-permute-start.5 = (f32[128,2,2048]{2,0,1:T(8,128)S(1)}, f32[128,2,2048]{2,0,1:T(8,128)S(1)}, u32[]{:S(2)}, u32[]{:S(2)}) collective-permute-start(f32[128,2,2048]{2,0,1:T(8,128)S(1)} %fusion.25), channel_id=1, source_target_pairs={{4,0},{8,4},{12,8},{16,12},{20,16},{24,20},{28,24},{5,1},{9,5},{13... | collective-permute-start | bytes 6291464 | tf_op jit(solution)/shard_map/ppermute | solution.py:15
  294.2 45.6 %collective-permute-start.6 = (f32[128,2,2048]{2,0,1:T(8,128)S(1)}, f32[128,2,2048]{2,0,1:T(8,128)S(1)}, u32[]{:S(2)}, u32[]{:S(2)}) collective-permute-start(f32[128,2,2048]{2,0,1:T(8,128)S(1)} %fusion.28), channel_id=1, source_target_pairs={{4,0},{8,4},{12,8},{16,12},{20,16},{24,20},{28,24},{5,1},{9,5},{13... | collective-permute-start | bytes 6291464 | tf_op jit(solution)/shard_map/ppermute | solution.py:15
  340.1 47.3 %copy-start.2 = (bf16[640,1,2048]{0,2,1:T(8,128)(2,1)S(1)}, bf16[640,1,2048]{0,2,1:T(8,128)(2,1)}, u32[]{:S(2)}) copy-start(bf16[640,1,2048]{0,2,1:T(8,128)(2,1)} %copy.62) | copy-start | bytes 7864324
  340.1 47.3 %copy-start.3 = (bf16[16,128,640]{2,1,0:T(8,128)(2,1)S(1)}, bf16[16,128,640]{2,1,0:T(8,128)(2,1)}, u32[]{:S(2)}) copy-start(bf16[16,128,640]{2,1,0:T(8,128)(2,1)} %fusion.2) | copy-start | bytes 7864324
  340.1 44.4 %collective-permute-start.7 = (f32[128,2,2048]{2,0,1:T(8,128)S(1)}, f32[128,2,2048]{2,0,1:T(8,128)S(1)}, u32[]{:S(2)}, u32[]{:S(2)}) collective-permute-start(f32[128,2,2048]{2,0,1:T(8,128)S(1)} %fusion.31), channel_id=1, source_target_pairs={{4,0},{8,4},{12,8},{16,12},{20,16},{24,20},{28,24},{5,1},{9,5},{13... | collective-permute-start | bytes 6291464 | tf_op jit(solution)/shard_map/ppermute | solution.py:15
  386.1 43.2 %collective-permute-start.8 = (f32[128,2,2048]{2,0,1:T(8,128)}, f32[128,2,2048]{2,0,1:T(8,128)}, u32[]{:S(2)}, u32[]{:S(2)}) collective-permute-start(f32[128,2,2048]{2,0,1:T(8,128)} %fusion.23), channel_id=1, source_target_pairs={{4,0},{8,4},{12,8},{16,12},{20,16},{24,20},{28,24},{5,1},{9,5},{13... | collective-permute-start | bytes 6291464 | tf_op jit(solution)/shard_map/ppermute | solution.py:15
  392.0 39.8 %copy-start.1 = (f32[128,1,2048]{2,0,1:T(8,128)S(1)}, f32[128,1,2048]{2,0,1:T(8,128)}, u32[]{:S(2)}) copy-start(f32[128,1,2048]{2,0,1:T(8,128)} %copy.75) | copy-start | bytes 3145732
  435.5 8.3 %collective-permute-start.9 = (f32[6,3,2048]{2,0,1:T(8,128)S(1)}, f32[6,3,2048]{2,0,1:T(8,128)S(1)}, u32[]{:S(2)}, u32[]{:S(2)}) collective-permute-start(f32[6,3,2048]{2,0,1:T(8,128)S(1)} %fusion.45), channel_id=1, source_target_pairs={{4,0},{8,4},{12,8},{16,12},{20,16},{24,20},{28,24},{5,1},{9,5},{13... | collective-permute-start | bytes 442376 | tf_op jit(solution)/shard_map/ppermute | solution.py:15
  436.8 0.7 copy-start.10
  437.5 6.6 %copy-start.12 = (f32[3,1,2048]{2,0,1:T(4,128)S(1)}, f32[3,1,2048]{2,0,1:T(4,128)}, u32[]{:S(2)}) copy-start(f32[3,1,2048]{2,0,1:T(4,128)} %copy-done.11) | copy-start | bytes 73732
  446.8 6.5 %copy-start.16 = (f32[3,2048]{1,0:T(4,128)S(1)}, f32[3,2048]{1,0:T(4,128)}, u32[]{:S(2)}) copy-start(f32[3,2048]{1,0:T(4,128)} %get-tuple-element.17) | copy-start | bytes 73732
  446.8 7.2 %copy-start.15 = (f32[3,2048]{1,0:T(4,128)S(1)}, f32[3,2048]{1,0:T(4,128)}, u32[]{:S(2)}) copy-start(f32[3,2048]{1,0:T(4,128)} %get-tuple-element.16) | copy-start | bytes 73732
  446.8 7.8 %copy-start.14 = (f32[3,2048]{1,0:T(4,128)S(1)}, f32[3,2048]{1,0:T(4,128)}, u32[]{:S(2)}) copy-start(f32[3,2048]{1,0:T(4,128)} %get-tuple-element.15) | copy-start | bytes 73732
  449.5 5.7 %copy-start.8 = (bf16[128,16,128]{0,2,1:T(8,128)(2,1)S(1)}, bf16[128,16,128]{0,2,1:T(8,128)(2,1)}, u32[]{:S(2)}) copy-start(bf16[128,16,128]{0,2,1:T(8,128)(2,1)} %get-tuple-element.41) | copy-start | bytes 1572868
  449.5 82.8 %all-to-all-start.1 = ((bf16[128,3,2048]{2,1,0:T(4,128)(2,1)}), bf16[128,3,2048]{2,1,0:T(4,128)(2,1)S(1)}, u32[]{:S(2)}, u32[]{:S(2)}) async-start(bf16[128,3,2048]{2,1,0:T(4,128)(2,1)} %copy.76), calls=%async_computation.1 | async-start | bytes 4194304 | tf_op jit(solution)/shard_map/all_to_all | solution.py:115
  453.3 77.4 %all-reduce.2.cloned.1.call-start = ((), (), s32[]{:S(2)}) async-start(), calls=%async_computation.2 | async-start | bytes 458752 | tf_op jit(solution)/shard_map/psum | solution.py:114
Sparse Core Ops, SparseCore 0:
  458.1 72.5 all-reduce.1
where the time goes:
time: 544 us; the launch traced here: 542 us
  waiting for transfers between devices  328 us (60%)
  local copies, waits for them, and re-layouts  114 us (21%)
  starting transfers between devices  42.9 us (8%)
  matrix products  22.2 us (4%)
  other arithmetic  20.2 us (4%)
  between operations  14.5 us (3%)
    ppermute x10, waiting for transfers between devices, from_behind(): lax.ppermute(value, axis, [(source, source + steps) for source in range(f...  234 us
    psum x1, waiting for transfers between devices, shards(): filter_grad = lax.psum(tap_terms, 'ctx')  74.4 us
    unnamed x63, local copies, waits for them, and re-layouts  44.5 us
    ppermute x10, starting transfers between devices, from_behind(): lax.ppermute(value, axis, [(source, source + steps) for source in range(f...  34.8 us
    another operation x3, local copies, waits for them, and re-layouts, shards(): jnp.stack([key_part.reshape(reach, tokens, width), value_part.reshape(rea...  22 us
    all_to_all x1, waiting for transfers between devices, shards(): local = lax.all_to_all(qkv, 'tp', split_axis=2, concat_axis=0, tiled=True)  19.9 us
  transfers between devices with their start and end apart: 13, of which 12 were waited for; matrix products, arithmetic and copies ran while one was open for 5% of the time, Pallas kernels for 0%

commit v1 on v0

--- a/solution.py
+++ b/solution.py
@@ -7,6 +7,15 @@
 KW = 7
 BLOCK = 128
 STEPS = 4
+
+
+def sum_by_hops(block, name):
+    n_dev = lax.axis_size(name)
+    result, hop = (block, 1)
+    while hop < n_dev:
+        result = result + lax.ppermute(result, name, [(i, i ^ hop) for i in range(n_dev)])
+        hop = 2 * hop
+    return result
 
 
 def from_behind(value, axis, steps):
@@ -111,7 +120,7 @@
         ],
         axis=1,
     )
-    filter_grad = lax.psum(tap_terms, "ctx")
+    filter_grad = sum_by_hops(tap_terms, "ctx")
     qkv_grad = lax.all_to_all(
         input_grad.astype(jnp.bfloat16), "tp", split_axis=0, concat_axis=2, tiled=True
     )

time: 544 us -> 481 us (0.88)
  waiting for transfers between devices: 328 us -> 274 us
  between operations: 14.5 us -> 1.11 us
  starting transfers between devices: 42.9 us -> 50.1 us
    psum x1 -> x0, waiting for transfers between devices: 74.4 us -> none  [shards(): filter_grad = lax.psum(tap_terms, 'ctx')]
    ppermute x0 -> x3, waiting for transfers between devices: none -> 20.7 us  [sum_by_hops(): lax.ppermute(result, name, [(i, i ^ hop) for i in range(n_dev)])]
    ppermute x0 -> x3, starting transfers between devices: none -> 7.28 us  [sum_by_hops(): lax.ppermute(result, name, [(i, i ^ hop) for i in range(n_dev)])]
  transfers between devices with their start and end apart: 13 -> 15, of which waited for: 12 -> 14; matrix products, arithmetic and copies ran while one was open for 5% -> 5% of each run, Pallas kernels for 0% -> 0%
where the time goes in v1:
time: 481 us; the launch traced here: 479 us
  waiting for transfers between devices  274 us (57%)
  local copies, waits for them, and re-layouts  111 us (23%)
  starting transfers between devices  50.1 us (10%)
  matrix products  22.2 us (5%)
  other arithmetic  20.4 us (4%)
    ppermute x10, waiting for transfers between devices, from_behind(): lax.ppermute(value, axis, [(source, source + steps) for source in range(f...  233 us
    unnamed x63, local copies, waits for them, and re-layouts  42.4 us
    ppermute x10, starting transfers between devices, from_behind(): lax.ppermute(value, axis, [(source, source + steps) for source in range(f...  34.8 us
    another operation x3, local copies, waits for them, and re-layouts, shards(): jnp.stack([key_part.reshape(reach, tokens, width), value_part.reshape(rea...  21.9 us
    ppermute x3, waiting for transfers between devices, sum_by_hops(): lax.ppermute(result, name, [(i, i ^ hop) for i in range(n_dev)])  20.7 us
    all_to_all x1, waiting for transfers between devices, shards(): local = lax.all_to_all(qkv, 'tp', split_axis=2, concat_axis=0, tiled=True)  19.9 us
    all_to_all x1, local copies, waits for them, and re-layouts, shards(): local = lax.all_to_all(qkv, 'tp', split_axis=2, concat_axis=0, tiled=True)  10.5 us
    slice x2, local copies, waits for them, and re-layouts, shards(): keys = joined[:, 0].reshape(reach * tokens, heads, HEAD_DIM)  10.1 us
  transfers between devices with their start and end apart: 15, of which 14 were waited for; matrix products, arithmetic and copies ran while one was open for 5% of the time, Pallas kernels for 0%

profile of v1, /device:TPU:0, one launch (start us, length us, event | category | flops | bytes accessed | tf_op | source)
XLA Modules:
  0.0 479.3 jit_solution(15907256021810353618)
XLA Ops:
  0.6 10.6 %copy.57 = bf16[32,3,8192]{0,1,2:T(4,128)(2,1)} copy(bf16[32,3,8192]{2,0,1:T(8,128)(2,1)} %param.4) | data formatting | bytes 3145728 | tf_op args[0]
  11.3 8.4 %reshape.158 = bf16[4,2,98304]{2,1,0:T(2,128)(2,1)} reshape(bf16[8192,3,32]{2,1,0:T(4,128)(2,1)} %bitcast.114) | data formatting | bytes 3145728
  19.6 4.3 all-to-all-start
  24.2 19.9 %all-to-all-done = bf16[4,2,98304]{2,1,0:T(2,128)(2,1)S(1)} async-done(((bf16[4,2,98304]{2,1,0:T(2,128)(2,1)}), bf16[4,2,98304]{2,1,0:T(2,128)(2,1)S(1)}, u32[]{:S(2)}, u32[]{:S(2)}) %all-to-all-start) | async-done | bytes 1572896 | tf_op jit(solution)/shard_map/all_to_all | solution.py:34
  44.1 7.1 %reshape.159 = bf16[8192,3,32]{2,1,0:T(4,128)(2,1)} reshape(bf16[4,2,98304]{2,1,0:T(2,128)(2,1)S(1)} %all-to-all-done) | data formatting | bytes 3145728
  51.1 10.5 %copy.59 = bf16[4,32,3,2048]{3,1,0,2:T(8,128)(2,1)S(1)} copy(bf16[4,32,3,2048]{1,2,3,0:T(4,128)(2,1)} %bitcast.113) | data formatting | bytes 3145728 | tf_op jit(solution)/shard_map/all_to_all | solution.py:34
  61.7 4.2 collective-permute-start
  66.0 2.1 collective-permute-done
  70.0 2.6 add_convert_fusion
  75.0 5.3 %collective-permute-start.1 = (bf16[128,2,2048]{2,0,1:T(8,128)(2,1)S(1)}, bf16[128,2,2048]{2,0,1:T(8,128)(2,1)}, u32[]{:S(2)}, u32[]{:S(2)}) collective-permute-start(bf16[128,2,2048]{2,0,1:T(8,128)(2,1)S(1)} %get-tuple-element.24), channel_id=1, source_target_pairs={{0,4},{4,8},{8,12},{12,16},{16,20},{20,24},{24,28},{1,5},{5,9},{9,... | collective-permute-start | bytes 3145736 | tf_op jit(solution)/shard_map/ppermute | solution.py:24
  80.3 20.0 %collective-permute-done.1 = bf16[128,2,2048]{2,0,1:T(8,128)(2,1)} collective-permute-done((bf16[128,2,2048]{2,0,1:T(8,128)(2,1)S(1)}, bf16[128,2,2048]{2,0,1:T(8,128)(2,1)}, u32[]{:S(2)}, u32[]{:S(2)}) %collective-permute-start.1) | collective-permute-done | bytes 1048608 | tf_op jit(solution)/shard_map/ppermute | solution.py:24
  100.3 5.5 %collective-permute-start.2 = (bf16[128,2,2048]{2,0,1:T(8,128)(2,1)}, bf16[128,2,2048]{2,0,1:T(8,128)(2,1)}, u32[]{:S(2)}, u32[]{:S(2)}) collective-permute-start(bf16[128,2,2048]{2,0,1:T(8,128)(2,1)} %collective-permute-done.1), channel_id=1, source_target_pairs={{0,4},{4,8},{8,12},{12,16},{16,20},{20,24},{24,28},{1,5},{5,9},{9,... | collective-permute-start | bytes 3145736 | tf_op jit(solution)/shard_map/ppermute | solution.py:24
  106.3 18.9 %collective-permute-done.2 = bf16[128,2,2048]{2,0,1:T(8,128)(2,1)} collective-permute-done((bf16[128,2,2048]{2,0,1:T(8,128)(2,1)}, bf16[128,2,2048]{2,0,1:T(8,128)(2,1)}, u32[]{:S(2)}, u32[]{:S(2)}) %collective-permute-start.2) | collective-permute-done | bytes 1048608 | tf_op jit(solution)/shard_map/ppermute | solution.py:24
  125.3 6.2 %collective-permute-start.3 = (bf16[128,2,2048]{2,0,1:T(8,128)(2,1)}, bf16[128,2,2048]{2,0,1:T(8,128)(2,1)}, u32[]{:S(2)}, u32[]{:S(2)}) collective-permute-start(bf16[128,2,2048]{2,0,1:T(8,128)(2,1)} %collective-permute-done.2), channel_id=1, source_target_pairs={{0,4},{4,8},{8,12},{12,16},{16,20},{20,24},{24,28},{1,5},{5,9},{9,... | collective-permute-start | bytes 3145736 | tf_op jit(solution)/shard_map/ppermute | solution.py:24
  135.5 14.5 %collective-permute-done.3 = bf16[128,2,2048]{2,0,1:T(8,128)(2,1)} collective-permute-done((bf16[128,2,2048]{2,0,1:T(8,128)(2,1)}, bf16[128,2,2048]{2,0,1:T(8,128)(2,1)}, u32[]{:S(2)}, u32[]{:S(2)}) %collective-permute-start.3) | collective-permute-done | bytes 1048608 | tf_op jit(solution)/shard_map/ppermute | solution.py:24
  150.0 6.4 %collective-permute-start.4 = (bf16[128,2,2048]{2,0,1:T(8,128)(2,1)}, bf16[128,2,2048]{2,0,1:T(8,128)(2,1)}, u32[]{:S(2)}, u32[]{:S(2)}) collective-permute-start(bf16[128,2,2048]{2,0,1:T(8,128)(2,1)} %collective-permute-done.3), channel_id=1, source_target_pairs={{0,4},{4,8},{8,12},{12,16},{16,20},{20,24},{24,28},{1,5},{5,9},{9,... | collective-permute-start | bytes 3145736 | tf_op jit(solution)/shard_map/ppermute | solution.py:24
  164.3 2.3 constant_dynamic-update-slice_fusion.3
  166.6 2.3 constant_dynamic-update-slice_fusion.2
  169.0 2.3 constant_dynamic-update-slice_fusion.1
  171.3 2.6 collective-permute-done.4
  173.9 2.3 constant_dynamic-update-slice_fusion
  176.2 5.7 %fusion.48 = (bf16[640,1,2048]{2,0,1:T(8,128)(2,1)}, bf16[640,1,2048]{2,0,1:T(8,128)(2,1)}) fusion(bf16[640,2,2048]{2,0,1:T(8,128)(2,1)} %constant_dynamic-update-slice_fusion), kind=kLoop, calls=%fused_computation.106 | loop fusion | bytes 10485760 | tf_op jit(solution)/shard_map/slice | solution.py:56
  181.9 4.4 copy.62
  186.3 4.5 copy.60
  190.8 6.6 %fusion.52 = (f32[16,128]{1,0:T(8,128)S(1)}, f32[16,128,640]{2,1,0:T(8,128)}) fusion(pred[128,640]{1,0:T(8,128)(4,1)} %and_and_fusion, bf16[128,16,128]{0,2,1:T(8,128)(2,1)} %bitcast.124, bf16[640,16,128]{0,2,1:T(8,128)(2,1)} %bitcast.115), kind=kOutput, calls=%fused_computation.110 | convolution fusion | flops 342098560 | bytes 8478720 | tf_op jit(solution)/shard_map/sub | solution.py:80
  197.4 4.1 fusion.18
  204.3 2.6 fusion.2
  206.9 5.4 %copy.72 = f32[640,16,128]{2,1,0:T(8,128)} copy(f32[640,16,128]{2,0,1:T(8,128)S(1)} %fusion.18) | data formatting | bytes 10485760 | tf_op jit(solution)/shard_map/hqk,qhd->khd/transpose | solution.py:89
  212.2 6.8 %stack_reshape.7 = f32[5,128,1,2048]{3,1,0,2:T(8,128)} reshape(f32[640,16,128]{2,1,0:T(8,128)} %copy.72) | data formatting | bytes 10485760 | tf_op jit(solution)/shard_map/stack;reshape | solution.py:104
  219.0 5.0 %convolution_bitcast_fusion = f32[640,16,128]{0,2,1:T(8,128)} fusion(bf16[128,16,128]{0,2,1:T(8,128)(2,1)} %bitcast.125, bf16[16,128,640]{2,1,0:T(8,128)(2,1)} %fusion.2), kind=kOutput, calls=%fused_computation.48 | convolution fusion | flops 335544320 | bytes 8388608 | tf_op jit(solution)/shard_map/hqk,qhd->khd/dot_general | solution.py:101
  224.0 7.3 %reshape.152 = f32[5,128,1,2048]{1,0,3,2:T(8,128)} reshape(f32[640,16,128]{0,2,1:T(8,128)} %convolution_bitcast_fusion) | data formatting | bytes 10485760 | tf_op jit(solution)/shard_map/stack;reshape | solution.py:104
  231.4 7.8 %copy.73 = f32[5,128,1,2048]{3,1,2,0:T(8,128)} copy(f32[5,128,1,2048]{1,0,3,2:T(8,128)} %reshape.152) | data formatting | bytes 10485760 | tf_op jit(solution)/shard_map/stack;reshape | solution.py:104
  242.6 44.7 %collective-permute-done.5 = f32[128,2,2048]{2,0,1:T(8,128)S(1)} collective-permute-done((f32[128,2,2048]{2,0,1:T(8,128)S(1)}, f32[128,2,2048]{2,0,1:T(8,128)S(1)}, u32[]{:S(2)}, u32[]{:S(2)}) %collective-permute-start.5) | collective-permute-done | bytes 2097184 | tf_op jit(solution)/shard_map/ppermute | solution.py:24
  289.2 44.1 %collective-permute-done.6 = f32[128,2,2048]{2,0,1:T(8,128)S(1)} collective-permute-done((f32[128,2,2048]{2,0,1:T(8,128)S(1)}, f32[128,2,2048]{2,0,1:T(8,128)S(1)}, u32[]{:S(2)}, u32[]{:S(2)}) %collective-permute-start.6) | collective-permute-done | bytes 2097184 | tf_op jit(solution)/shard_map/ppermute | solution.py:24
  335.2 42.9 %collective-permute-done.7 = f32[128,2,2048]{2,0,1:T(8,128)S(1)} collective-permute-done((f32[128,2,2048]{2,0,1:T(8,128)S(1)}, f32[128,2,2048]{2,0,1:T(8,128)S(1)}, u32[]{:S(2)}, u32[]{:S(2)}) %collective-permute-start.7) | collective-permute-done | bytes 2097184 | tf_op jit(solution)/shard_map/ppermute | solution.py:24
  383.0 2.5 copy.75
  385.5 37.3 %collective-permute-done.8 = f32[128,2,2048]{2,0,1:T(8,128)} collective-permute-done((f32[128,2,2048]{2,0,1:T(8,128)}, f32[128,2,2048]{2,0,1:T(8,128)}, u32[]{:S(2)}, u32[]{:S(2)}) %collective-permute-start.8) | collective-permute-done | bytes 2097184 | tf_op jit(solution)/shard_map/ppermute | solution.py:24
  422.9 2.5 fusion.33
  425.4 3.6 multiply_reduce_fusion
  431.1 6.2 %collective-permute-done.9 = f32[6,3,2048]{2,0,1:T(8,128)S(1)} collective-permute-done((f32[6,3,2048]{2,0,1:T(8,128)S(1)}, f32[6,3,2048]{2,0,1:T(8,128)S(1)}, u32[]{:S(2)}, u32[]{:S(2)}) %collective-permute-start.9) | collective-permute-done | bytes 147488 | tf_op jit(solution)/shard_map/ppermute | solution.py:24
  437.7 2.6 fusion.5
  440.4 2.7 copy.76
  443.1 3.7 all-to-all-start.1
  446.9 3.0 collective-permute-start.10
  449.9 6.2 %collective-permute-done.10 = f32[3,7,2048]{2,0,1:T(4,128)S(1)} collective-permute-done((f32[3,7,2048]{2,0,1:T(4,128)S(1)}, f32[3,7,2048]{2,0,1:T(4,128)S(1)}, u32[]{:S(2)}, u32[]{:S(2)}) %collective-permute-start.10) | collective-permute-done | bytes 172064 | tf_op jit(solution)/shard_map/ppermute | solution.py:16
  457.8 5.8 %collective-permute-done.11 = f32[3,7,2048]{2,0,1:T(4,128)S(1)} collective-permute-done((f32[3,7,2048]{2,0,1:T(4,128)S(1)}, f32[3,7,2048]{2,0,1:T(4,128)S(1)}, u32[]{:S(2)}, u32[]{:S(2)}) %collective-permute-start.11) | collective-permute-done | bytes 172064 | tf_op jit(solution)/shard_map/ppermute | solution.py:16
  463.7 2.7 collective-permute-start.12
  467.3 8.7 %collective-permute-done.12 = f32[3,7,2048]{2,0,1:T(4,128)S(1)} collective-permute-done((f32[3,7,2048]{2,0,1:T(4,128)S(1)}, f32[3,7,2048]{2,0,1:T(4,128)S(1)}, u32[]{:S(2)}, u32[]{:S(2)}) %collective-permute-start.12) | collective-permute-done | bytes 172064 | tf_op jit(solution)/shard_map/ppermute | solution.py:16
  (97 shorter events, 40.1 us)
Async XLA Ops:
  19.6 4.3 copy-start.14
  19.6 24.4 %all-to-all-start = ((bf16[4,2,98304]{2,1,0:T(2,128)(2,1)}), bf16[4,2,98304]{2,1,0:T(2,128)(2,1)S(1)}, u32[]{:S(2)}, u32[]{:S(2)}) async-start(bf16[4,2,98304]{2,1,0:T(2,128)(2,1)} %reshape.158), calls=%async_computation | async-start | bytes 3145728 | tf_op jit(solution)/shard_map/all_to_all | solution.py:34
  61.7 4.3 copy-start.5
  61.7 6.4 %collective-permute-start = (bf16[6,3,2048]{2,0,1:T(8,128)(2,1)S(1)}, bf16[6,3,2048]{2,0,1:T(8,128)(2,1)S(1)}, u32[]{:S(2)}, u32[]{:S(2)}) collective-permute-start(bf16[6,3,2048]{2,0,1:T(8,128)(2,1)S(1)} %slice.138), channel_id=1, source_target_pairs={{0,4},{4,8},{8,12},{12,16},{16,20},{20,24},{24,28},{1,5},{5,9},{9,... | collective-permute-start | bytes 221192 | tf_op jit(solution)/shard_map/ppermute | solution.py:24
  66.0 6.7 %copy-start.12 = (f32[3,1,2048]{2,0,1:T(4,128)}, f32[3,1,2048]{2,0,1:T(4,128)S(1)}, u32[]{:S(2)}) copy-start(f32[3,1,2048]{2,0,1:T(4,128)S(1)} %copy.107) | copy-start | bytes 73732
  72.7 1.1 copy-start.6
  73.8 57.7 %copy-start.17 = (s32[8]{0:T(128)S(1)}, s32[8]{0:T(128)}, u32[]{:S(2)}) copy-start(s32[8]{0:T(128)} %param.6) | copy-start | bytes 100
  75.0 25.4 %collective-permute-start.1 = (bf16[128,2,2048]{2,0,1:T(8,128)(2,1)S(1)}, bf16[128,2,2048]{2,0,1:T(8,128)(2,1)}, u32[]{:S(2)}, u32[]{:S(2)}) collective-permute-start(bf16[128,2,2048]{2,0,1:T(8,128)(2,1)S(1)} %get-tuple-element.24), channel_id=1, source_target_pairs={{0,4},{4,8},{8,12},{12,16},{16,20},{20,24},{24,28},{1,5},{5,9},{9,... | collective-permute-start | bytes 3145736 | tf_op jit(solution)/shard_map/ppermute | solution.py:24
  100.3 24.9 %collective-permute-start.2 = (bf16[128,2,2048]{2,0,1:T(8,128)(2,1)}, bf16[128,2,2048]{2,0,1:T(8,128)(2,1)}, u32[]{:S(2)}, u32[]{:S(2)}) collective-permute-start(bf16[128,2,2048]{2,0,1:T(8,128)(2,1)} %collective-permute-done.1), channel_id=1, source_target_pairs={{0,4},{4,8},{8,12},{12,16},{16,20},{20,24},{24,28},{1,5},{5,9},{9,... | collective-permute-start | bytes 3145736 | tf_op jit(solution)/shard_map/ppermute | solution.py:24
  125.3 24.7 %collective-permute-start.3 = (bf16[128,2,2048]{2,0,1:T(8,128)(2,1)}, bf16[128,2,2048]{2,0,1:T(8,128)(2,1)}, u32[]{:S(2)}, u32[]{:S(2)}) collective-permute-start(bf16[128,2,2048]{2,0,1:T(8,128)(2,1)} %collective-permute-done.2), channel_id=1, source_target_pairs={{0,4},{4,8},{8,12},{12,16},{16,20},{20,24},{24,28},{1,5},{5,9},{9,... | collective-permute-start | bytes 3145736 | tf_op jit(solution)/shard_map/ppermute | solution.py:24
  150.0 23.9 %collective-permute-start.4 = (bf16[128,2,2048]{2,0,1:T(8,128)(2,1)}, bf16[128,2,2048]{2,0,1:T(8,128)(2,1)}, u32[]{:S(2)}, u32[]{:S(2)}) collective-permute-start(bf16[128,2,2048]{2,0,1:T(8,128)(2,1)} %collective-permute-done.3), channel_id=1, source_target_pairs={{0,4},{4,8},{8,12},{12,16},{16,20},{20,24},{24,28},{1,5},{5,9},{9,... | collective-permute-start | bytes 3145736 | tf_op jit(solution)/shard_map/ppermute | solution.py:24
  197.4 4.1 copy-start.4
  197.4 5.0 %copy-start.7 = (f32[16,128,640]{2,1,0:T(8,128)S(1)}, f32[16,128,640]{2,1,0:T(8,128)}, u32[]{:S(2)}) copy-start(f32[16,128,640]{2,1,0:T(8,128)} %get-tuple-element.39) | copy-start | bytes 15728644
  197.4 5.0 %copy-start.9 = (bf16[128,2048]{0,1:T(8,128)(2,1)S(1)}, bf16[128,2048]{0,1:T(8,128)(2,1)}, u32[]{:S(2)}) copy-start(bf16[128,2048]{0,1:T(8,128)(2,1)} %copy.65) | copy-start | bytes 1572868
  239.2 48.1 %slice-start = ((s8[5242880]{0:T(1024)(128)(4,1)}), s8[4194304]{0:T(1024)(128)(4,1)S(1)}, s32[]{:S(2)}) async-start(s8[5242880]{0:T(1024)(128)(4,1)} %bitcast.108), calls=%async_computation.2 | async-start | bytes 8388608
  239.2 48.1 %slice-start.1 = ((s8[5242880]{0:T(1024)(128)(4,1)}), s8[1048576]{0:T(1024)(128)(4,1)S(1)}, s32[]{:S(2)}) async-start(s8[5242880]{0:T(1024)(128)(4,1)} %bitcast.108), calls=%async_computation.3 | async-start | bytes 2097152
  239.2 48.1 %copy-start = (f32[5,128,1,2048]{3,1,2,0:T(8,128)S(1)}, f32[5,128,1,2048]{3,1,2,0:T(8,128)}, u32[]{:S(2)}) copy-start(f32[5,128,1,2048]{3,1,2,0:T(8,128)} %copy.73) | copy-start | bytes 15728644
  241.0 46.3 %collective-permute-start.5 = (f32[128,2,2048]{2,0,1:T(8,128)S(1)}, f32[128,2,2048]{2,0,1:T(8,128)S(1)}, u32[]{:S(2)}, u32[]{:S(2)}) collective-permute-start(f32[128,2,2048]{2,0,1:T(8,128)S(1)} %fusion.25), channel_id=1, source_target_pairs={{4,0},{8,4},{12,8},{16,12},{20,16},{24,20},{28,24},{5,1},{9,5},{13... | collective-permute-start | bytes 6291464 | tf_op jit(solution)/shard_map/ppermute | solution.py:24
  287.7 45.6 %collective-permute-start.6 = (f32[128,2,2048]{2,0,1:T(8,128)S(1)}, f32[128,2,2048]{2,0,1:T(8,128)S(1)}, u32[]{:S(2)}, u32[]{:S(2)}) collective-permute-start(f32[128,2,2048]{2,0,1:T(8,128)S(1)} %fusion.28), channel_id=1, source_target_pairs={{4,0},{8,4},{12,8},{16,12},{20,16},{24,20},{28,24},{5,1},{9,5},{13... | collective-permute-start | bytes 6291464 | tf_op jit(solution)/shard_map/ppermute | solution.py:24
  333.6 47.3 %copy-start.2 = (bf16[640,1,2048]{0,2,1:T(8,128)(2,1)S(1)}, bf16[640,1,2048]{0,2,1:T(8,128)(2,1)}, u32[]{:S(2)}) copy-start(bf16[640,1,2048]{0,2,1:T(8,128)(2,1)} %copy.62) | copy-start | bytes 7864324
  333.6 47.3 %copy-start.3 = (bf16[16,128,640]{2,1,0:T(8,128)(2,1)S(1)}, bf16[16,128,640]{2,1,0:T(8,128)(2,1)}, u32[]{:S(2)}) copy-start(bf16[16,128,640]{2,1,0:T(8,128)(2,1)} %fusion.2) | copy-start | bytes 7864324
  333.6 44.4 %collective-permute-start.7 = (f32[128,2,2048]{2,0,1:T(8,128)S(1)}, f32[128,2,2048]{2,0,1:T(8,128)S(1)}, u32[]{:S(2)}, u32[]{:S(2)}) collective-permute-start(f32[128,2,2048]{2,0,1:T(8,128)S(1)} %fusion.31), channel_id=1, source_target_pairs={{4,0},{8,4},{12,8},{16,12},{20,16},{24,20},{28,24},{5,1},{9,5},{13... | collective-permute-start | bytes 6291464 | tf_op jit(solution)/shard_map/ppermute | solution.py:24
  379.6 43.3 %collective-permute-start.8 = (f32[128,2,2048]{2,0,1:T(8,128)}, f32[128,2,2048]{2,0,1:T(8,128)}, u32[]{:S(2)}, u32[]{:S(2)}) collective-permute-start(f32[128,2,2048]{2,0,1:T(8,128)} %fusion.23), channel_id=1, source_target_pairs={{4,0},{8,4},{12,8},{16,12},{20,16},{24,20},{28,24},{5,1},{9,5},{13... | collective-permute-start | bytes 6291464 | tf_op jit(solution)/shard_map/ppermute | solution.py:24
  385.5 39.9 %copy-start.1 = (f32[128,1,2048]{2,0,1:T(8,128)S(1)}, f32[128,1,2048]{2,0,1:T(8,128)}, u32[]{:S(2)}) copy-start(f32[128,1,2048]{2,0,1:T(8,128)} %copy.75) | copy-start | bytes 3145732
  429.0 8.3 %collective-permute-start.9 = (f32[6,3,2048]{2,0,1:T(8,128)S(1)}, f32[6,3,2048]{2,0,1:T(8,128)S(1)}, u32[]{:S(2)}, u32[]{:S(2)}) collective-permute-start(f32[6,3,2048]{2,0,1:T(8,128)S(1)} %fusion.45), channel_id=1, source_target_pairs={{4,0},{8,4},{12,8},{16,12},{20,16},{24,20},{28,24},{5,1},{9,5},{13... | collective-permute-start | bytes 442376 | tf_op jit(solution)/shard_map/ppermute | solution.py:24
  430.4 0.7 copy-start.10
  431.1 6.6 %copy-start.13 = (f32[3,1,2048]{2,0,1:T(4,128)S(1)}, f32[3,1,2048]{2,0,1:T(4,128)}, u32[]{:S(2)}) copy-start(f32[3,1,2048]{2,0,1:T(4,128)} %copy-done.12) | copy-start | bytes 73732
  440.3 6.5 %copy-start.11 = (f32[3,7,2048]{2,0,1:T(4,128)S(1)}, f32[3,7,2048]{2,0,1:T(4,128)}, u32[]{:S(2)}) copy-start(f32[3,7,2048]{2,0,1:T(4,128)} %copy-done.10) | copy-start | bytes 516100
  440.4 6.5 %copy-start.16 = (f32[3,2048]{1,0:T(4,128)S(1)}, f32[3,2048]{1,0:T(4,128)}, u32[]{:S(2)}) copy-start(f32[3,2048]{1,0:T(4,128)} %get-tuple-element.16) | copy-start | bytes 73732
  440.4 6.5 %copy-start.15 = (f32[3,2048]{1,0:T(4,128)S(1)}, f32[3,2048]{1,0:T(4,128)}, u32[]{:S(2)}) copy-start(f32[3,2048]{1,0:T(4,128)} %get-tuple-element.15) | copy-start | bytes 73732
  443.1 23.3 %copy-start.8 = (bf16[128,16,128]{0,2,1:T(8,128)(2,1)S(1)}, bf16[128,16,128]{0,2,1:T(8,128)(2,1)}, u32[]{:S(2)}) copy-start(bf16[128,16,128]{0,2,1:T(8,128)(2,1)} %get-tuple-element.41) | copy-start | bytes 1572868
  443.1 33.8 %all-to-all-start.1 = ((bf16[128,3,2048]{2,1,0:T(4,128)(2,1)}), bf16[128,3,2048]{2,1,0:T(4,128)(2,1)S(1)}, u32[]{:S(2)}, u32[]{:S(2)}) async-start(bf16[128,3,2048]{2,1,0:T(4,128)(2,1)} %copy.76), calls=%async_computation.1 | async-start | bytes 4194304 | tf_op jit(solution)/shard_map/all_to_all | solution.py:124
  446.9 9.2 %collective-permute-start.10 = (f32[3,7,2048]{2,0,1:T(4,128)S(1)}, f32[3,7,2048]{2,0,1:T(4,128)S(1)}, u32[]{:S(2)}, u32[]{:S(2)}) collective-permute-start(f32[3,7,2048]{2,0,1:T(4,128)S(1)} %bitcast_dynamic-update-slice_fusion), channel_id=1, source_target_pairs={{0,4},{4,0},{8,12},{12,8},{16,20},{20,16},{24,28},{28,24},{1,5},{5... | collective-permute-start | bytes 516104 | tf_op jit(solution)/shard_map/ppermute | solution.py:16
  456.1 7.4 %collective-permute-start.11 = (f32[3,7,2048]{2,0,1:T(4,128)S(1)}, f32[3,7,2048]{2,0,1:T(4,128)S(1)}, u32[]{:S(2)}, u32[]{:S(2)}) collective-permute-start(f32[3,7,2048]{2,0,1:T(4,128)S(1)} %add.139), channel_id=1, source_target_pairs={{0,8},{4,12},{8,0},{12,4},{16,24},{20,28},{24,16},{28,20},{1,9},{5... | collective-permute-start | bytes 516104 | tf_op jit(solution)/shard_map/ppermute | solution.py:16
  463.7 12.4 %collective-permute-start.12 = (f32[3,7,2048]{2,0,1:T(4,128)S(1)}, f32[3,7,2048]{2,0,1:T(4,128)S(1)}, u32[]{:S(2)}, u32[]{:S(2)}) collective-permute-start(f32[3,7,2048]{2,0,1:T(4,128)S(1)} %add.140), channel_id=1, source_target_pairs={{0,16},{4,20},{8,24},{12,28},{16,0},{20,4},{24,8},{28,12},{1,17},{... | collective-permute-start | bytes 516104 | tf_op jit(solution)/shard_map/ppermute | solution.py:16
